TPU v7x, 512 devices: a whole 4x8x8 slice. The times are simulated.
512 devices in a mesh: seq: 64 (over z, x, core), head: 8 (over y).
Axes of the slice: x: 4, y: 8, z: 8, core: 2. Of those that a mesh axis runs over, the one named last changes fastest.
Arguments:
- xbc: bfloat16 [24576, 10240], P('seq', 'head'), may hold values from -6 to 6
- gate_z: bfloat16 [24576, 8192], P('seq', 'head'), may hold values from -6 to 6
- dt_raw: bfloat16 [128, 24576], P('head', 'seq'), may hold values from -3 to 3
- dt_bias: float32 [128], P('head'), may hold values from -1 to 0.5
- a_log: float32 [128], P('head'), may hold values from -11.5 to -6.6
- skip_d: float32 [128], P('head'), may hold values from 0.5 to 1.5
- conv_weight: float32 [4, 10240], P(None, 'head'), may hold values from -3 to 3
- conv_bias: float32 [10240], P('head'), may hold values from -3 to 3
- norm_gain: float32 [8192], P('head'), may hold values from 0.1 to 1.9
- out_weight: bfloat16 [8192, 4096], P('head', 'seq'), may hold values from -0.1875 to 0.1875
- starts: int32 [24576], P('seq'), may hold values from 0 to 1, as said below
Outputs:
- mixed: bfloat16 [24576, 4096], P('seq', 'head')
Inputs may be any that keep to these rules, and one draw needn't show every extreme that they name: `starts`: a 0 or 1 flag for every token; every 1 lies among the first 6144 tokens, and there is at least one.
All inputs are finite; a program needn't handle non-finite values.
Results may differ from a plain program's by a relative error of at most 0.013.
Values may be sent and summed in bfloat16 or wider, within the bound.
A program may use at most 128 MiB of HBM per device.

v0:
```python
import jax
import jax.numpy as jnp
from jax import lax
from jax.sharding import PartitionSpec as P

P_SIZE = 64
N = 128
DI = 8192
HG = 16
GW = 1280


def carried_in(part, axis, combine, identity):
    place = lax.axis_index(axis)
    gathered = jax.tree.map(lambda a: lax.all_gather(a, axis), part)
    state = jax.tree.map(lambda a, e: jnp.zeros_like(a) + jnp.asarray(e, a.dtype), part, identity)

    def one(hop, state):
        return combine(
            state, jax.tree.map(lambda a: lax.dynamic_index_in_dim(a, hop, 0, False), gathered)
        )

    return lax.fori_loop(0, place, one, state)


def passed_along(block, axis, distance):
    devices = range(lax.axis_size(axis))
    route = [(i - distance, i) for i in devices if i - distance in devices]
    return lax.ppermute(block, axis, route)


def combine(earlier, later):
    return (earlier[0] * later[0], later[0][:, None, None] * earlier[1] + later[1])


def chain_states(decays, states):
    identity = (jnp.ones_like(decays), jnp.zeros_like(states))
    result = carried_in((decays, states), "seq", combine, identity)
    return result[1]


def block_local(item):
    xc, bc, cc, dtc, lc, sc = item
    cumul = jnp.cumsum(lc, axis=1)
    runs = jnp.cumsum(sc)
    tail = (
        jnp.where(
            (runs == runs[-1])[None, :], jnp.exp(jnp.minimum(cumul[:, -1:] - cumul, 0.0)), 0.0
        )
        * dtc
    )
    b_heads = jnp.repeat(bc, HG, axis=1)
    scaled = (tail[:, :, None] * jnp.swapaxes(b_heads, 0, 1).astype(jnp.float32)).astype(
        jnp.bfloat16
    )
    local = jnp.einsum("shp,hsn->hpn", xc, scaled, preferred_element_type=jnp.float32)
    total = jnp.exp(cumul[:, -1]) * (runs[-1] == 0).astype(jnp.float32)
    enter = jnp.exp(cumul) * (runs == 0).astype(jnp.float32)[None, :]
    return (local, total, enter)


def block_inner(item):
    xc, bc, cc, dtc, lc, sc = item
    length = xc.shape[0]
    cumul = jnp.cumsum(lc, axis=1)
    runs = jnp.cumsum(sc)
    lower = jnp.arange(length)[:, None] >= jnp.arange(length)[None, :]
    same = lower & (runs[:, None] == runs[None, :])
    diff = cumul[:, :, None] - cumul[:, None, :]
    wdec = jnp.where(same[None], jnp.exp(jnp.minimum(diff, 0.0)), 0.0)
    scores = jnp.einsum("tgn,sgn->gts", cc, bc, preferred_element_type=jnp.float32)
    scores_h = jnp.repeat(scores, HG, axis=0)
    weights = (scores_h * wdec * dtc[:, None, :]).astype(jnp.bfloat16)
    return jnp.einsum("hts,shp->thp", weights, xc, preferred_element_type=jnp.float32)


def body(
    xbc,
    gate_z,
    dt_raw,
    dt_bias,
    a_log,
    skip_d,
    conv_weight,
    conv_bias,
    norm_gain,
    out_weight,
    starts,
):
    tok = xbc.shape[0]
    width = conv_weight.shape[0]
    chans = xbc.shape[1]
    groups = chans // GW
    heads = dt_raw.shape[0]
    rim, rim_flags = passed_along(
        (xbc[tok - (width - 1) :], starts[tok - (width - 1) :].astype(jnp.bfloat16)), "seq", 1
    )
    flags_int = rim_flags.astype(jnp.int32)
    after_rim = jnp.sum(flags_int) - jnp.cumsum(flags_int)
    counts = jnp.cumsum(starts)
    padded = jnp.concatenate([rim, xbc], axis=0).astype(jnp.float32)
    count_ext = jnp.concatenate([-after_rim, counts])
    acc = conv_bias[None, :] + conv_weight[width - 1][None, :] * xbc.astype(jnp.float32)
    for lag in range(1, width):
        shifted = padded[width - 1 - lag : width - 1 - lag + tok]
        keep = (count_ext[width - 1 - lag : width - 1 - lag + tok] == counts).astype(jnp.float32)
        acc = acc + conv_weight[width - 1 - lag][None, :] * shifted * keep[:, None]
    unit = jax.nn.silu(acc).astype(jnp.bfloat16)
    grid = unit.reshape(tok, groups, GW)
    xs = grid[:, :, : HG * P_SIZE].reshape(tok, heads, P_SIZE)
    bmat = grid[:, :, HG * P_SIZE : HG * P_SIZE + N]
    cmat = grid[:, :, HG * P_SIZE + N :]
    steps_dt = jax.nn.softplus(dt_raw.astype(jnp.float32) + dt_bias[:, None])
    logs = -jnp.exp(a_log)[:, None] * steps_dt
    length = min(128, tok)
    nblocks = tok // length
    x_blocks = xs.reshape(nblocks, length, heads, P_SIZE)
    b_blocks = bmat.reshape(nblocks, length, groups, N)
    c_blocks = cmat.reshape(nblocks, length, groups, N)
    dt_blocks = steps_dt.reshape(heads, nblocks, length).transpose(1, 0, 2)
    log_blocks = logs.reshape(heads, nblocks, length).transpose(1, 0, 2)
    start_blocks = starts.reshape(nblocks, length)
    items = (x_blocks, b_blocks, c_blocks, dt_blocks, log_blocks, start_blocks)

    def fold(carry, item):
        local, total = item
        return ((carry[0] * total, carry[1] * total[:, None, None] + local), None)

    y_diag, (locals_all, totals, enters) = lax.map(
        lambda item: (block_inner(item), block_local(item)), items
    )
    init = (jnp.ones((heads,), jnp.float32), jnp.zeros((heads, P_SIZE, N), jnp.float32))
    result, unused = lax.scan(fold, init, (locals_all, totals))
    entering = chain_states(result[0], result[1])

    def apply(state, item):
        cc, enter, local, total = item
        c_heads = jnp.repeat(cc, HG, axis=1)
        y_off = (
            jnp.einsum(
                "thn,hpn->thp",
                c_heads,
                state.astype(jnp.bfloat16),
                preferred_element_type=jnp.float32,
            )
            * enter.T[:, :, None]
        )
        return (state * total[:, None, None] + local, y_off)

    unused_state, y_offs = lax.scan(apply, entering, (c_blocks, enters, locals_all, totals))
    y_all = (y_diag + y_offs).reshape(tok, heads, P_SIZE) + skip_d[None, :, None] * xs.astype(
        jnp.float32
    )
    gated = y_all.reshape(tok, heads * P_SIZE) * jax.nn.silu(gate_z.astype(jnp.float32))
    total_sq = lax.psum(jnp.sum(gated * gated, axis=1), "head")
    normed = (gated * lax.rsqrt(total_sq / DI + 1e-05)[:, None] * norm_gain[None, :]).astype(
        jnp.bfloat16
    )
    terms = jnp.dot(
        normed,
        lax.all_gather(out_weight, "seq", axis=1, tiled=True),
        preferred_element_type=jnp.float32,
    )
    return lax.psum_scatter(terms.astype(jnp.bfloat16), "head", scatter_dimension=1, tiled=True)


def solution(mesh):
    placed = (
        P("seq", "head"),
        P("seq", "head"),
        P("head", "seq"),
        P("head"),
        P("head"),
        P("head"),
        P(None, "head"),
        P("head"),
        P("head"),
        P("head", "seq"),
        P("seq"),
    )
    return jax.shard_map(
        body, mesh=mesh, in_specs=placed, out_specs=P("seq", "head"), check_vma=False
    )
```

profile of v0, /device:TPU:2, one launch (start us, length us, event | category | flops | bytes accessed | tf_op | source)
XLA Modules:
  0.0 368.8 jit_solution(15041050396364430548)
XLA Ops:
  7.3 1.9 collective-permute-start.1
  10.0 3.5 collective-permute-start
  19.0 1.4 maximum_convert_fusion
  20.5 1.9 fusion.44
  23.3 1.9 reshape.277
  25.2 2.0 copy.38
  27.2 1.3 broadcast.139.clone
  28.5 17.6 %while.53 = (s32[]{:T(128)}, f32[3,128,16,64]{1,3,2,0:T(8,128)}, f32[3,16,64,128]{3,2,1,0:T(8,128)S(1)}, f32[3,16]{1,0:T(4,128)S(1)}, f32[3,16,128]{2,1,0:T(8,12...) while((s32[]{:T(128)}, f32[3,128,16,64]{1,3,2,0:T(8,128)}, ...), condition=%wide.region_7.8_spmd, body=%wide.region_4.7_spmd.sunk | while | flops 73752848 | bytes 2099011 | solution.py:129
  33.0 1.4 fusion.75
  38.9 1.4 fusion.75
  44.7 1.4 fusion.75
  50.7 130.2 %all-reduce = f32[1024]{0:T(1024)S(1)} all-reduce(f32[1024]{0:T(1024)S(1)} %dynamic-update-slice), channel_id=2, replica_groups=mesh['seq'=64,'head'=8] {'seq'}, use_global_device_ids=true, to_apply=%add | all-reduce | flops 1024 | bytes 8192
  181.0 18.2 %all-gather.7.cloned.1.call-done = f32[1024,64,128]{2,1,0:T(8,128)} async-done(((f32[16,64,128]{2,1,0:T(8,128)}), f32[1024,64,128]{2,1,0:T(8,128)}) %all-gather.7.cloned.1.call-update) | async-done | bytes 33554448 | tf_op jit(solution)/shard_map/all_gather | solution.py:15
  199.3 2.5 while.54
  201.7 1.3 broadcast.139
  203.1 4.4 %while.55 = (s32[]{:T(128)}, f32[16,64,128]{2,1,0:T(8,128)S(1)}, f32[3,128,16,64]{1,3,2,0:T(8,128)}, f32[3,16]{1,0:T(4,128)S(1)}, f32[3,16,64,128]{3,2,1,0:T(8,1...) while((s32[]{:T(128)}, f32[16,64,128]{2,1,0:T(8,128)S(1)}, ...), condition=%wide.region_13.14_spmd, body=%wide.region_12.13_spmd.sunk | while | flops 34078720 | bytes 2745125 | solution.py:150
  207.5 3.4 add.93
  210.9 2.3 copy.48
  213.2 1.8 reshape.278
  215.0 2.6 multiply_reduce_fusion.1
  217.6 17.0 %psum.7 = f32[384]{0:T(512)S(1)} all-reduce(f32[384]{0:T(512)S(1)} %get-tuple-element.329), channel_id=1, replica_groups=mesh['seq'=64,'head'=8] {'head'}, use_global_device_ids=true, to_apply=%region_15.16 | all-reduce | flops 384 | bytes 3072 | tf_op jit(solution)/shard_map/psum | solution.py:155
  234.6 53.6 %all-gather.5.cloned.1.call-done = bf16[1024,4096]{0,1:T(8,128)(2,1)} async-done(((bf16[1024,64]{0,1:T(8,128)(2,1)}), bf16[1024,4096]{0,1:T(8,128)(2,1)}) %all-gather.5.cloned.1.call-update) | async-done | bytes 8388624 | tf_op jit(solution)/shard_map/all_gather | solution.py:161
  288.3 10.2 %convolution_convert_fusion = bf16[384,4096]{1,0:T(8,128)(2,1)} fusion(bf16[1024,4096]{0,1:T(8,128)(2,1)} %all-gather.5.cloned.1.call-done, f32[384,1024]{1,0:T(8,128)S(1)} %get-tuple-element.330, f32[1024]{0:T(1024)S(1)} %copy-done.5, f32[384]{0:T(512)S(1)} %add_rsqrt_fusion), kind=kOutput, calls=%fused_computation.59 | convolution fusion | flops 3223977984 | bytes 13112832 | tf_op jit(solution)/shard_map/dot_general | solution.py:159
  298.5 63.8 %reduce-scatter.2.cloned.1.call-done = bf16[384,512]{1,0:T(8,128)(2,1)} async-done(((bf16[384,4096]{1,0:T(8,128)(2,1)}), bf16[384,512]{1,0:T(8,128)(2,1)}) %reduce-scatter.2.cloned.1.call-update) | async-done | bytes 393232 | tf_op jit(solution)/shard_map/reduce_scatter | solution.py:164
  (128 shorter events, 30.2 us)
Async XLA Ops:
  6.5 192.7 %all-gather.7.cloned.1.call-start = ((), (), s32[]{:S(2)}) async-start(), calls=%async_computation.3 | async-start | bytes 34078720 | tf_op jit(solution)/shard_map/all_gather | solution.py:15
  7.3 10.0 %collective-permute-start.1 = (bf16[3]{0:T(256)(128)(2,1)S(1)}, bf16[3]{0:T(256)(128)(2,1)S(1)}, u32[]{:S(2)}, u32[]{:S(2)}) collective-permute-start(bf16[3]{0:T(256)(128)(2,1)S(1)} %slice.68), channel_id=1, source_target_pairs={{0,8},{8,16},{16,24},{24,32},{32,40},{40,48},{48,56},{56,64},{64,7... | collective-permute-start | bytes 26 | tf_op jit(solution)/shard_map/ppermute | solution.py:29
  10.0 9.1 %collective-permute-start = (bf16[3,1280]{1,0:T(4,128)(2,1)S(1)}, bf16[3,1280]{1,0:T(4,128)(2,1)S(1)}, u32[]{:S(2)}, u32[]{:S(2)}) collective-permute-start(bf16[3,1280]{1,0:T(4,128)(2,1)S(1)} %slice.66), channel_id=1, source_target_pairs={{0,8},{8,16},{16,24},{24,32},{32,40},{40,48},{48,56},{56,64},{64,7... | collective-permute-start | bytes 23048 | tf_op jit(solution)/shard_map/ppermute | solution.py:29
  17.2 3.2 copy-start.2
  17.2 3.2 copy-start.3
  22.3 1.0 copy-start.1
  46.1 2.1 copy-start.4
  46.6 0.8 copy-start
  47.5 240.8 %all-gather.5.cloned.1.call-start = ((), (), s32[]{:S(2)}) async-start(), calls=%async_computation.1 | async-start | bytes 8519680 | tf_op jit(solution)/shard_map/all_gather | solution.py:161
  48.2 314.0 %reduce-scatter.2.cloned.1.call-start = ((), (), s32[]{:S(2)}) async-start(), calls=%async_computation.2 | async-start | bytes 3538944 | tf_op jit(solution)/shard_map/reduce_scatter | solution.py:164
  215.0 73.2 %copy-start.5 = (f32[1024]{0:T(1024)S(1)}, f32[1024]{0:T(1024)}, u32[]{:S(2)}) copy-start(f32[1024]{0:T(1024)} %param.27) | copy-start | bytes 12292
Sparse Core Ops, SparseCore 0:
  47.6 151.5 all-gather.6
  202.6 85.6 all-gather.4
  298.6 63.6 reduce-scatter.1
where the time goes:
time: 372 us; the launch traced here: 369 us
  blocking collectives  147 us (40%)
  waiting for transfers between devices  136 us (37%)
  other arithmetic  22.4 us (6%)
  local copies, waits for them, and re-layouts  20.7 us (6%)
  matrix products  20.1 us (5%)
  between operations  14 us (4%)
  starting transfers between devices  5.48 us (1%)
    unnamed x1, blocking collectives  130 us
    reduce_scatter x1, waiting for transfers between devices, body(): lax.psum_scatter(terms.astype(jnp.bfloat16), 'head', scatter_dimension=1,...  63.8 us
    all_gather x1, waiting for transfers between devices, body(): lax.all_gather(out_weight, 'seq', axis=1, tiled=True)  53.6 us
    all_gather x1, waiting for transfers between devices, carried_in(): gathered = jax.tree.map(lambda a: lax.all_gather(a, axis), part)  18.2 us
    psum x1, blocking collectives, body(): total_sq = lax.psum(jnp.sum(gated * gated, axis=1), 'head')  17 us
    dot_general x1, matrix products, body(): jnp.dot(normed, lax.all_gather(out_weight, 'seq', axis=1, tiled=True), pr...  10.2 us
  transfers between devices with their start and end apart: 5, of which 3 were waited for; matrix products, arithmetic and copies ran while one was open for 7% of the time, Pallas kernels for 0%

commit v1 on v0

--- a/solution.py
+++ b/solution.py
@@ -152,7 +152,7 @@
         jnp.float32
     )
     gated = y_all.reshape(tok, heads * P_SIZE) * jax.nn.silu(gate_z.astype(jnp.float32))
-    total_sq = lax.psum(jnp.sum(gated * gated, axis=1), "head")
+    total_sq = jnp.sum(lax.all_gather(jnp.sum(gated * gated, axis=1), "head"), axis=0)
     normed = (gated * lax.rsqrt(total_sq / DI + 1e-05)[:, None] * norm_gain[None, :]).astype(
         jnp.bfloat16
     )

time: 372 us -> 379 us (1.019)
  the two profiles are of different devices: /device:TPU:2 before, /device:TPU:6 now
where the time goes in v1:
time: 379 us; the launch traced here: 375 us
  blocking collectives  143 us (38%)
  waiting for transfers between devices  141 us (37%)
  other arithmetic  27.1 us (7%)
  local copies, waits for them, and re-layouts  20.7 us (5%)
  matrix products  20.1 us (5%)
  between operations  14.1 us (4%)
  starting transfers between devices  6.28 us (2%)
    unnamed x1, blocking collectives  119 us
    reduce_scatter x1, waiting for transfers between devices, body(): lax.psum_scatter(terms.astype(jnp.bfloat16), 'head', scatter_dimension=1,...  70.7 us
    all_gather x1, waiting for transfers between devices, body(): lax.all_gather(out_weight, 'seq', axis=1, tiled=True)  41.7 us
    all_gather x1, waiting for transfers between devices, carried_in(): gathered = jax.tree.map(lambda a: lax.all_gather(a, axis), part)  27.7 us
    all_gather x1, blocking collectives, body(): lax.all_gather(jnp.sum(gated * gated, axis=1), 'head')  23.8 us
    dot_general x1, matrix products, body(): jnp.dot(normed, lax.all_gather(out_weight, 'seq', axis=1, tiled=True), pr...  10.2 us
  transfers between devices with their start and end apart: 5, of which 3 were waited for; matrix products, arithmetic and copies ran while one was open for 8% of the time, Pallas kernels for 0%

profile of v1, /device:TPU:6, one launch (start us, length us, event | category | flops | bytes accessed | tf_op | source)
XLA Modules:
  0.0 375.0 jit_solution(14710446757673591819)
XLA Ops:
  7.3 1.9 collective-permute-start.1
  10.0 4.3 %collective-permute-start = (bf16[3,1280]{1,0:T(4,128)(2,1)S(1)}, bf16[3,1280]{1,0:T(4,128)(2,1)S(1)}, u32[]{:S(2)}, u32[]{:S(2)}) collective-permute-start(bf16[3,1280]{1,0:T(4,128)(2,1)S(1)} %slice.66), channel_id=1, source_target_pairs={{0,8},{8,16},{16,24},{24,32},{32,40},{40,48},{48,56},{56,64},{64,7... | collective-permute-start | bytes 23048 | tf_op jit(solution)/shard_map/ppermute | solution.py:29
  19.8 1.4 maximum_convert_fusion
  21.3 1.9 fusion.44
  24.1 1.9 reshape.285
  26.0 2.0 copy.38
  28.0 1.3 broadcast.146.clone
  29.3 17.6 %while.53 = (s32[]{:T(128)}, f32[3,128,16,64]{1,3,2,0:T(8,128)}, f32[3,16,64,128]{3,2,1,0:T(8,128)S(1)}, f32[3,16]{1,0:T(4,128)S(1)}, f32[3,16,128]{2,1,0:T(8,12...) while((s32[]{:T(128)}, f32[3,128,16,64]{1,3,2,0:T(8,128)}, ...), condition=%wide.region_7.8_spmd, body=%wide.region_4.7_spmd.sunk | while | flops 73752848 | bytes 2099011 | solution.py:129
  33.8 1.4 fusion.75
  39.7 1.4 fusion.75
  45.5 1.4 fusion.75
  51.5 119.4 %all-reduce = f32[1024]{0:T(1024)S(1)} all-reduce(f32[1024]{0:T(1024)S(1)} %dynamic-update-slice), channel_id=2, replica_groups=mesh['seq'=64,'head'=8] {'seq'}, use_global_device_ids=true, to_apply=%add | all-reduce | flops 1024 | bytes 8192
  171.0 27.7 %all-gather.9.cloned.1.call-done = f32[1024,64,128]{2,1,0:T(8,128)} async-done(((f32[16,64,128]{2,1,0:T(8,128)}), f32[1024,64,128]{2,1,0:T(8,128)}) %all-gather.9.cloned.1.call-update) | async-done | bytes 33554448 | tf_op jit(solution)/shard_map/all_gather | solution.py:15
  198.7 7.4 %while.54 = (s32[]{:T(128)}, f32[16,64,128]{2,1,0:T(8,128)S(1)}, s32[]{:T(128)}, f32[64,16]{1,0:T(8,128)S(1)}, f32[64,16,64,128]{3,2,1,0:T(8,128)}, /*index=5*/s32[]{:T(128)}, s32[]{:T(128)}, s32[]{:T(128)}) while((s32[]{:T(128)}, f32[16,64,128]{2,1,0:T(8,128)S(1)}, s32[]{:T(128)}, f32[64,16]{1,0:T(8,128)S(1)}, ...), condition=%wide.region_11.12_spmd, body=%wide.region_10.11_spmd.sunk | while | flops 262149 | bytes 1573183 | solution.py:23
  206.1 1.3 broadcast.146
  207.5 4.4 %while.55 = (s32[]{:T(128)}, f32[16,64,128]{2,1,0:T(8,128)S(1)}, f32[3,128,16,64]{1,3,2,0:T(8,128)}, f32[3,16]{1,0:T(4,128)S(1)}, f32[3,16,64,128]{3,2,1,0:T(8,1...) while((s32[]{:T(128)}, f32[16,64,128]{2,1,0:T(8,128)S(1)}, ...), condition=%wide.region_13.14_spmd, body=%wide.region_12.13_spmd.sunk | while | flops 34078720 | bytes 2745125 | solution.py:150
  211.9 3.4 add.95
  215.3 2.3 copy.48
  217.6 1.8 reshape.286
  219.4 2.5 multiply_reduce_fusion.1
  222.0 23.8 %all-gather.3 = f32[8,1,384]{2,1,0:T(1,128)S(1)} all-gather(f32[1,1,384]{2,1,0:T(1,128)S(1)} %reshape.280), channel_id=4, replica_groups=mesh['seq'=64,'head'=8] {'head'}, dimensions={0}, use_global_device_ids=true | all-gather | bytes 13824 | tf_op jit(solution)/shard_map/all_gather | solution.py:155
  245.9 41.7 %all-gather.7.cloned.1.call-done = bf16[1024,4096]{0,1:T(8,128)(2,1)} async-done(((bf16[1024,64]{0,1:T(8,128)(2,1)}), bf16[1024,4096]{0,1:T(8,128)(2,1)}) %all-gather.7.cloned.1.call-update) | async-done | bytes 8388624 | tf_op jit(solution)/shard_map/all_gather | solution.py:161
  287.6 10.2 %convolution_convert_fusion = bf16[384,4096]{1,0:T(8,128)(2,1)} fusion(bf16[1024,4096]{0,1:T(8,128)(2,1)} %all-gather.7.cloned.1.call-done, f32[384,1024]{1,0:T(8,128)S(1)} %get-tuple-element.330, f32[1024]{0:T(1024)S(1)} %copy-done.5, f32[384]{0:T(512)S(1)} %add_rsqrt_fusion), kind=kOutput, calls=%fused_computation.59 | convolution fusion | flops 3223977984 | bytes 13112832 | tf_op jit(solution)/shard_map/dot_general | solution.py:159
  297.8 70.7 %reduce-scatter.2.cloned.1.call-done = bf16[384,512]{1,0:T(8,128)(2,1)} async-done(((bf16[384,4096]{1,0:T(8,128)(2,1)}), bf16[384,512]{1,0:T(8,128)(2,1)}) %reduce-scatter.2.cloned.1.call-update) | async-done | bytes 393232 | tf_op jit(solution)/shard_map/reduce_scatter | solution.py:164
  (138 shorter events, 35.1 us)
Async XLA Ops:
  6.5 192.1 %all-gather.9.cloned.1.call-start = ((), (), s32[]{:S(2)}) async-start(), calls=%async_computation.3 | async-start | bytes 34078720 | tf_op jit(solution)/shard_map/all_gather | solution.py:15
  7.3 10.8 %collective-permute-start.1 = (bf16[3]{0:T(256)(128)(2,1)S(1)}, bf16[3]{0:T(256)(128)(2,1)S(1)}, u32[]{:S(2)}, u32[]{:S(2)}) collective-permute-start(bf16[3]{0:T(256)(128)(2,1)S(1)} %slice.68), channel_id=1, source_target_pairs={{0,8},{8,16},{16,24},{24,32},{32,40},{40,48},{48,56},{56,64},{64,7... | collective-permute-start | bytes 26 | tf_op jit(solution)/shard_map/ppermute | solution.py:29
  10.0 9.9 %collective-permute-start = (bf16[3,1280]{1,0:T(4,128)(2,1)S(1)}, bf16[3,1280]{1,0:T(4,128)(2,1)S(1)}, u32[]{:S(2)}, u32[]{:S(2)}) collective-permute-start(bf16[3,1280]{1,0:T(4,128)(2,1)S(1)} %slice.66), channel_id=1, source_target_pairs={{0,8},{8,16},{16,24},{24,32},{32,40},{40,48},{48,56},{56,64},{64,7... | collective-permute-start | bytes 23048 | tf_op jit(solution)/shard_map/ppermute | solution.py:29
  18.0 3.2 copy-start.2
  18.0 3.2 copy-start.3
  23.1 1.0 copy-start.1
  46.9 2.1 copy-start.4
  47.4 0.8 copy-start
  48.3 239.3 %all-gather.7.cloned.1.call-start = ((), (), s32[]{:S(2)}) async-start(), calls=%async_computation.1 | async-start | bytes 8519680 | tf_op jit(solution)/shard_map/all_gather | solution.py:161
  49.0 319.5 %reduce-scatter.2.cloned.1.call-start = ((), (), s32[]{:S(2)}) async-start(), calls=%async_computation.2 | async-start | bytes 3538944 | tf_op jit(solution)/shard_map/reduce_scatter | solution.py:164
  219.4 68.2 %copy-start.5 = (f32[1024]{0:T(1024)S(1)}, f32[1024]{0:T(1024)}, u32[]{:S(2)}) copy-start(f32[1024]{0:T(1024)} %param.27) | copy-start | bytes 12292
Sparse Core Ops, SparseCore 0:
  48.4 150.2 all-gather.8
  202.0 85.5 all-gather.6
  297.9 70.5 reduce-scatter.1
